TPU v7x, 512 devices: a whole 4x8x8 slice. The times are simulated.
512 devices in a mesh: dp: 16 (over x_lo, y), peak: 16 (over z, x_hi), mod: 2 (over core).
Axes of the slice: x: 4 (x_hi: 2, x_lo: 2; x = x_hi * 2 + x_lo), y: 8, z: 8, core: 2. Of those that a mesh axis runs over, the one named last changes fastest.
Arguments:
- hidden_in: bfloat16 [2, 49152, 1024], P('mod', ('dp', 'peak')), parts along dimension 1, may hold values from -31 to 31
- value_bins: int32 [2, 49152], P('mod', ('dp', 'peak')), parts along dimension 1, may hold values from 0 to 50
- mask_flags: int32 [2, 49152], P('mod', ('dp', 'peak')), parts along dimension 1, may hold values 0 or 1
- segment_ids: int32 [2, 256, 192], P('mod', ('dp', 'peak')), parts along dimension 1, may hold values from 0 to 3, never falling along the last dimension, each value on 1 to 96 neighbouring positions
- bin_table: bfloat16 [2, 51, 1024], P('mod'), may hold values from -3 to 3
- mask_vector: bfloat16 [2, 1024], P('mod'), may hold values from -4 to 4
- qkv_weight: bfloat16 [1024, 3072], P('mod'), may hold values from -1 to 1
- out_weight: bfloat16 [1024, 1024], P('mod'), may hold values from -1.5 to 1.5
Outputs:
- update: bfloat16 [2, 49152, 1024], P('mod', ('dp', 'peak')), parts along dimension 1
There are 16 independent parts, one for each index of `dp`. A program takes and returns all parts, laid end to end along the dimension named above; an argument that names none is the same for every part. Nothing has to cross between parts.
Inputs may be any that keep to these rules, and one draw needn't show every extreme that they name: `segment_ids`: in each block of 192 tokens the segments 0 to 3 follow in order, each of 1 to 96 tokens, one of exactly 96.
All inputs are finite; a program needn't handle non-finite values. No bound on the sum of `mask_flags` on one device may be relied on, other than what follows from the above.
Results may differ from a plain program's by a relative error of at most 0.01205.
The roundings to bfloat16 on the way count: a program that leaves them out, or rounds other values in their place, can miss the bound.
Values may be sent and summed in bfloat16 or wider, within the bound.
A program may use at most 128 MiB of HBM per device.

v0:
```python
import math

import jax
import jax.numpy as jnp
from jax import lax
from jax.sharding import PartitionSpec as P

H = 16
NBINS = 51
SEG_DEV = 4


def from_partner(value, axis, bit):
    mask = 2**bit
    pairs = [(source, source ^ mask) for source in range(lax.axis_size(axis))]
    return lax.ppermute(value, axis, pairs)


def attend_block(running, queries, key_block, value_block, score_bias, score_scale):
    row_max, denominator, numerator = running
    scores = (
        jnp.einsum("thd,khd->thk", queries, key_block, preferred_element_type=jnp.float32)
        * score_scale
        + score_bias
    )
    new_max = jnp.maximum(row_max, jnp.max(scores, axis=2))
    correction = jnp.exp(row_max - new_max)
    weights = jnp.exp(scores - new_max[:, :, None])
    denominator = denominator * correction + jnp.sum(weights, axis=2)
    numerator = numerator * correction[:, :, None] + jnp.einsum(
        "thk,khd->thd",
        weights.astype(jnp.bfloat16),
        value_block,
        preferred_element_type=jnp.float32,
    )
    return (new_max, denominator, numerator)


def shards(
    hidden_in, value_bins, mask_flags, segment_ids, bin_table, mask_vector, qkv_weight, out_weight
):
    tok_count = hidden_in.shape[1]
    width = hidden_in.shape[2]
    head_count = H
    head_size = width // head_count
    score_scale = float(head_size) ** (-0.5)
    selector = (value_bins[0][:, None] == jnp.arange(NBINS, dtype=jnp.int32)[None, :]).astype(
        jnp.bfloat16
    )
    bin_rows = jnp.dot(selector, bin_table[0], preferred_element_type=jnp.float32)
    chosen = jnp.where(
        mask_flags[0][:, None] == 1,
        mask_vector[0][None, :].astype(jnp.float32),
        hidden_in[0].astype(jnp.float32),
    )
    embedded = (chosen + bin_rows).astype(jnp.bfloat16)
    columns = embedded
    projected = jnp.dot(
        columns,
        lax.all_gather(qkv_weight, "mod", axis=0, tiled=True),
        preferred_element_type=jnp.float32,
    )
    projected = projected.astype(jnp.bfloat16).reshape(tok_count, head_count, 3, head_size)
    key_values = projected[:, :, 1:3, :].reshape(tok_count, 2 * width)
    seg_select = (
        segment_ids[0, 0][None, :] == jnp.arange(SEG_DEV, dtype=jnp.int32)[:, None]
    ).astype(jnp.bfloat16)
    pooled_sums = jnp.dot(seg_select, key_values, preferred_element_type=jnp.float32)
    counts = jnp.sum(seg_select.astype(jnp.float32), axis=1)
    pooled = (pooled_sums / counts[:, None]).astype(jnp.bfloat16)
    pool_bias = jnp.broadcast_to(
        jnp.log(counts).astype(jnp.bfloat16)[:, None], (SEG_DEV, head_count)
    )
    partner_kv, partner_bias = from_partner((pooled, pool_bias), "mod", 0)
    queries = projected[:, :, 0, :]
    start_state = (
        jnp.full((tok_count, head_count), -1e30, jnp.float32),
        jnp.zeros((tok_count, head_count), jnp.float32),
        jnp.zeros((tok_count, head_count, head_size), jnp.float32),
    )
    portion = lax.all_gather(key_values, "peak", axis=0, tiled=True)
    row_count = portion.shape[0]
    unpacked = portion.reshape(row_count, head_count, 2, head_size)
    block_size = math.gcd(row_count, 512)

    def one_step(index, state):
        sliced = lax.dynamic_slice_in_dim(unpacked, index * block_size, block_size, 0)
        return attend_block(state, queries, sliced[:, :, 0], sliced[:, :, 1], 0.0, score_scale)

    running = lax.fori_loop(0, row_count // block_size, one_step, start_state)
    kv_part = lax.all_gather(partner_kv, "peak", axis=0, tiled=True)
    bias_part = lax.all_gather(partner_bias, "peak", axis=0, tiled=True)
    row_count = kv_part.shape[0]
    fold_unpacked = kv_part.reshape(row_count, head_count, 2, head_size)
    score_bias = jnp.transpose(bias_part.astype(jnp.float32))[None, :, :]
    row_max, denominator, numerator = attend_block(
        running, queries, fold_unpacked[:, :, 0], fold_unpacked[:, :, 1], score_bias, score_scale
    )
    attended = (numerator / denominator[:, :, None]).astype(jnp.bfloat16).reshape(tok_count, width)
    columns = attended
    result = jnp.dot(
        columns,
        lax.all_gather(out_weight, "mod", axis=0, tiled=True),
        preferred_element_type=jnp.float32,
    )
    return result.astype(jnp.bfloat16).reshape(1, tok_count, width)


def solution(mesh):
    placed = (
        P("mod", ("dp", "peak"), None),
        P("mod", ("dp", "peak")),
        P("mod", ("dp", "peak")),
        P("mod", ("dp", "peak"), None),
        P("mod", None, None),
        P("mod", None),
        P("mod", None),
        P("mod", None),
    )
    return jax.shard_map(
        shards,
        mesh=mesh,
        in_specs=placed,
        out_specs=P("mod", ("dp", "peak"), None),
        check_vma=False,
    )
```

profile of v0, /device:TPU:1, one launch (start us, length us, event | category | flops | bytes accessed | tf_op | source)
XLA Modules:
  0.0 342.8 jit_solution(13260755747699797976)
XLA Ops:
  6.5 0.7 all-gather.6.cloned.1.call-update
  7.3 0.0 all-gather.8.cloned.1.call-start
  7.3 0.7 broadcast_in_dim.57
  8.0 0.7 compare_reduce_fusion
  8.7 32.6 %all-gather.6.cloned.1.call-done = bf16[1024,3072]{1,0:T(8,128)(2,1)} async-done(((bf16[512,3072]{1,0:T(8,128)(2,1)}), bf16[1024,3072]{1,0:T(8,128)(2,1)}) %all-gather.6.cloned.1.call-update) | async-done | bytes 6291472 | tf_op jit(solution)/shard_map/all_gather | solution.py:60
  41.3 4.5 %convolution_convert_fusion = bf16[192,3072]{1,0:T(8,128)(2,1)S(1)} fusion(bf16[1024,3072]{1,0:T(8,128)(2,1)} %all-gather.6.cloned.1.call-done, bf16[1,192,1024]{2,1,0:T(8,128)(2,1)} %param.10, f32[1024]{0:T(1024)S(1)} %bitcast.108, pred[192]{0:T(512)(128)(4,1)S(1)} %compare_reduce_fusion, bf16[1,51,1024]{2,1,0:T(8,128)(2,1)S(1)} %copy-done, s32[192]{0:T(256)} %bitcast.112), kind=kOutput, calls=%fused_computation.21 | convolution fusion | flops 1229399552 | bytes 7973824 | tf_op jit(solution)/shard_map/dot_general | solution.py:58
  45.8 1.6 copy.34
  47.4 1.3 slice.32
  48.7 1.2 copy.35
  50.0 0.0 all-gather.10.cloned.1.call-start
  50.0 0.1 convert_reduce_fusion
  50.2 0.1 broadcast_in_dim.56
  50.2 2.1 collective-permute-start.1
  52.4 0.9 collective-permute-done.1
  53.3 33.7 %all-gather.1 = bf16[16,4,16]{2,1,0:T(4,128)(2,1)S(1)} all-gather(bf16[1,4,16]{2,1,0:T(4,128)(2,1)S(1)} %bitcast.111), channel_id=1, replica_groups=mesh['dp'=16,'peak'=16,'mod'=2] {'peak'}, dimensions={0}, use_global_device_ids=true | all-gather | bytes 2176 | tf_op jit(solution)/shard_map/all_gather | solution.py:92
  87.0 0.1 copy.40
  87.0 0.4 fusion.18
  87.4 9.4 %collective-permute-start = (bf16[4,2048]{1,0:T(4,128)(2,1)S(1)}, bf16[4,2048]{1,0:T(4,128)(2,1)S(1)}, u32[]{:S(2)}, u32[]{:S(2)}) collective-permute-start(bf16[4,2048]{1,0:T(4,128)(2,1)S(1)} %fusion.18), channel_id=1, source_target_pairs={{0,1},{1,0},{2,3},{3,2},{4,5},{5,4},{6,7},{7,6},{8,9},{9,8},{10,11... | collective-permute-start | bytes 49160 | tf_op jit(solution)/shard_map/ppermute | solution.py:16
  96.8 1.1 slice_bitcast_fusion
  97.9 31.0 %all-gather = bf16[16,4,2048]{2,1,0:T(4,128)(2,1)S(1)} all-gather(bf16[1,4,2048]{2,1,0:T(4,128)(2,1)S(1)} %bitcast.107), channel_id=1, replica_groups=mesh['dp'=16,'peak'=16,'mod'=2] {'peak'}, dimensions={0}, use_global_device_ids=true | all-gather | bytes 278528 | tf_op jit(solution)/shard_map/all_gather | solution.py:91
  128.8 0.4 reshape.45
  129.3 0.7 fusion.40
  130.0 1.1 copy.45
  131.1 1.4 fusion.41
  132.5 103.9 %all-gather.8.cloned.1.call-done = bf16[3072,2048]{1,0:T(8,128)(2,1)} async-done(((bf16[192,2048]{1,0:T(8,128)(2,1)}), bf16[3072,2048]{1,0:T(8,128)(2,1)}) %all-gather.8.cloned.1.call-update) | async-done | bytes 12582928 | tf_op jit(solution)/shard_map/all_gather | solution.py:81
  236.4 16.7 %copy.36 = bf16[3072,2048]{0,1:T(8,128)(2,1)} copy(bf16[3072,2048]{1,0:T(8,128)(2,1)} %all-gather.8.cloned.1.call-done) | data formatting | bytes 25165824 | tf_op jit(solution)/shard_map/all_gather | solution.py:81
  253.1 79.7 %while.18 = (s32[]{:T(128)}, f32[192,16]{0,1:T(8,128)S(1)}, f32[192,16]{0,1:T(8,128)S(1)}, f32[192,16,64]{0,2,1:T(8,128)S(1)}, bf16[3072,16,2,64]{0,3,2,1:T(8,12...) while((s32[]{:T(128)}, f32[192,16]{0,1:T(8,128)S(1)}, ...), condition=%wide.region_3.0_spmd.clone, body=%wide.region_0.3_spmd.clone.sunk | while | flops 415841280 | bytes 23134400 | solution.py:90
  253.1 4.9 %bitcast_reduce_fusion.2 = (f32[192,16]{0,1:T(8,128)S(1)}, f32[16,512,192]{1,2,0:T(8,128)}) fusion(bf16[192,16,64]{0,2,1:T(8,128)(2,1)S(1)} %get-tuple-element.258, bf16[3072,16,2,64]{0,3,2,1:T(8,128)(2,1)} %get-tuple-element.257, s32[]{:T(128)S(6)} %select_n.18), kind=kOutput, calls=%fused_computation.1.clone.1 | convolution fusion | flops 204469248 | bytes 7745540 | tf_op jit(solution)/shard_map/while/body/eval_jaxpr/thd,khd->thk/dot_general | solution.py:22
  258.0 3.6 %fusion.54 = f32[192,16]{0,1:T(8,128)S(1)} fusion(f32[16,512,192]{1,2,0:T(8,128)} %get-tuple-element.228, f32[192,16]{0,1:T(8,128)S(1)} %select_maximum_fusion.2), kind=kLoop, calls=%fused_computation.4.clone.1 | loop fusion | flops 4715520 | bytes 6316032 | tf_op jit(solution)/shard_map/while/body/eval_jaxpr/reduce_sum | solution.py:29
  261.7 4.7 %fusion.56 = f32[192,16,64]{0,2,1:T(8,128)S(1)} fusion(f32[16,512,192]{1,2,0:T(8,128)} %get-tuple-element.228, f32[192,16]{0,1:T(8,128)S(1)} %select_maximum_fusion.2, bf16[3072,16,2,64]{0,3,2,1:T(8,128)(2,1)} %get-tuple-element.257, s32[]{:T(128)S(6)} %select_n.18, s32[]{:T(128)S(6)} %add.95, f32[192,16,64]{0,2,1:T(8,128)S(1)} %get-tuple-element.245, ...), kind=kOutput, calls=%fused_computation.9.clone.1 | convolution fusion | flops 206635008 | bytes 8937481 | tf_op jit(solution)/shard_map/while/body/eval_jaxpr/thk,khd->thd/dot_general | solution.py:30
  266.4 4.9 %bitcast_reduce_fusion.2 = (f32[192,16]{0,1:T(8,128)S(1)}, f32[16,512,192]{1,2,0:T(8,128)}) fusion(bf16[192,16,64]{0,2,1:T(8,128)(2,1)S(1)} %get-tuple-element.258, bf16[3072,16,2,64]{0,3,2,1:T(8,128)(2,1)} %get-tuple-element.257, s32[]{:T(128)S(6)} %select_n.18), kind=kOutput, calls=%fused_computation.1.clone.1 | convolution fusion | flops 204469248 | bytes 7745540 | tf_op jit(solution)/shard_map/while/body/eval_jaxpr/thd,khd->thk/dot_general | solution.py:22
  271.3 3.6 %fusion.54 = f32[192,16]{0,1:T(8,128)S(1)} fusion(f32[16,512,192]{1,2,0:T(8,128)} %get-tuple-element.228, f32[192,16]{0,1:T(8,128)S(1)} %select_maximum_fusion.2), kind=kLoop, calls=%fused_computation.4.clone.1 | loop fusion | flops 4715520 | bytes 6316032 | tf_op jit(solution)/shard_map/while/body/eval_jaxpr/reduce_sum | solution.py:29
  274.9 4.7 %fusion.56 = f32[192,16,64]{0,2,1:T(8,128)S(1)} fusion(f32[16,512,192]{1,2,0:T(8,128)} %get-tuple-element.228, f32[192,16]{0,1:T(8,128)S(1)} %select_maximum_fusion.2, bf16[3072,16,2,64]{0,3,2,1:T(8,128)(2,1)} %get-tuple-element.257, s32[]{:T(128)S(6)} %select_n.18, s32[]{:T(128)S(6)} %add.95, f32[192,16,64]{0,2,1:T(8,128)S(1)} %get-tuple-element.245, ...), kind=kOutput, calls=%fused_computation.9.clone.1 | convolution fusion | flops 206635008 | bytes 8937481 | tf_op jit(solution)/shard_map/while/body/eval_jaxpr/thk,khd->thd/dot_general | solution.py:30
  279.6 4.9 %bitcast_reduce_fusion.2 = (f32[192,16]{0,1:T(8,128)S(1)}, f32[16,512,192]{1,2,0:T(8,128)}) fusion(bf16[192,16,64]{0,2,1:T(8,128)(2,1)S(1)} %get-tuple-element.258, bf16[3072,16,2,64]{0,3,2,1:T(8,128)(2,1)} %get-tuple-element.257, s32[]{:T(128)S(6)} %select_n.18), kind=kOutput, calls=%fused_computation.1.clone.1 | convolution fusion | flops 204469248 | bytes 7745540 | tf_op jit(solution)/shard_map/while/body/eval_jaxpr/thd,khd->thk/dot_general | solution.py:22
  284.5 3.6 %fusion.54 = f32[192,16]{0,1:T(8,128)S(1)} fusion(f32[16,512,192]{1,2,0:T(8,128)} %get-tuple-element.228, f32[192,16]{0,1:T(8,128)S(1)} %select_maximum_fusion.2), kind=kLoop, calls=%fused_computation.4.clone.1 | loop fusion | flops 4715520 | bytes 6316032 | tf_op jit(solution)/shard_map/while/body/eval_jaxpr/reduce_sum | solution.py:29
  288.2 4.7 %fusion.56 = f32[192,16,64]{0,2,1:T(8,128)S(1)} fusion(f32[16,512,192]{1,2,0:T(8,128)} %get-tuple-element.228, f32[192,16]{0,1:T(8,128)S(1)} %select_maximum_fusion.2, bf16[3072,16,2,64]{0,3,2,1:T(8,128)(2,1)} %get-tuple-element.257, s32[]{:T(128)S(6)} %select_n.18, s32[]{:T(128)S(6)} %add.95, f32[192,16,64]{0,2,1:T(8,128)S(1)} %get-tuple-element.245, ...), kind=kOutput, calls=%fused_computation.9.clone.1 | convolution fusion | flops 206635008 | bytes 8937481 | tf_op jit(solution)/shard_map/while/body/eval_jaxpr/thk,khd->thd/dot_general | solution.py:30
  292.9 4.9 %bitcast_reduce_fusion.2 = (f32[192,16]{0,1:T(8,128)S(1)}, f32[16,512,192]{1,2,0:T(8,128)}) fusion(bf16[192,16,64]{0,2,1:T(8,128)(2,1)S(1)} %get-tuple-element.258, bf16[3072,16,2,64]{0,3,2,1:T(8,128)(2,1)} %get-tuple-element.257, s32[]{:T(128)S(6)} %select_n.18), kind=kOutput, calls=%fused_computation.1.clone.1 | convolution fusion | flops 204469248 | bytes 7745540 | tf_op jit(solution)/shard_map/while/body/eval_jaxpr/thd,khd->thk/dot_general | solution.py:22
  297.8 3.6 %fusion.54 = f32[192,16]{0,1:T(8,128)S(1)} fusion(f32[16,512,192]{1,2,0:T(8,128)} %get-tuple-element.228, f32[192,16]{0,1:T(8,128)S(1)} %select_maximum_fusion.2), kind=kLoop, calls=%fused_computation.4.clone.1 | loop fusion | flops 4715520 | bytes 6316032 | tf_op jit(solution)/shard_map/while/body/eval_jaxpr/reduce_sum | solution.py:29
  301.5 4.7 %fusion.56 = f32[192,16,64]{0,2,1:T(8,128)S(1)} fusion(f32[16,512,192]{1,2,0:T(8,128)} %get-tuple-element.228, f32[192,16]{0,1:T(8,128)S(1)} %select_maximum_fusion.2, bf16[3072,16,2,64]{0,3,2,1:T(8,128)(2,1)} %get-tuple-element.257, s32[]{:T(128)S(6)} %select_n.18, s32[]{:T(128)S(6)} %add.95, f32[192,16,64]{0,2,1:T(8,128)S(1)} %get-tuple-element.245, ...), kind=kOutput, calls=%fused_computation.9.clone.1 | convolution fusion | flops 206635008 | bytes 8937481 | tf_op jit(solution)/shard_map/while/body/eval_jaxpr/thk,khd->thd/dot_general | solution.py:30
  306.2 4.9 %bitcast_reduce_fusion.2 = (f32[192,16]{0,1:T(8,128)S(1)}, f32[16,512,192]{1,2,0:T(8,128)}) fusion(bf16[192,16,64]{0,2,1:T(8,128)(2,1)S(1)} %get-tuple-element.258, bf16[3072,16,2,64]{0,3,2,1:T(8,128)(2,1)} %get-tuple-element.257, s32[]{:T(128)S(6)} %select_n.18), kind=kOutput, calls=%fused_computation.1.clone.1 | convolution fusion | flops 204469248 | bytes 7745540 | tf_op jit(solution)/shard_map/while/body/eval_jaxpr/thd,khd->thk/dot_general | solution.py:22
  311.1 3.6 %fusion.54 = f32[192,16]{0,1:T(8,128)S(1)} fusion(f32[16,512,192]{1,2,0:T(8,128)} %get-tuple-element.228, f32[192,16]{0,1:T(8,128)S(1)} %select_maximum_fusion.2), kind=kLoop, calls=%fused_computation.4.clone.1 | loop fusion | flops 4715520 | bytes 6316032 | tf_op jit(solution)/shard_map/while/body/eval_jaxpr/reduce_sum | solution.py:29
  314.8 4.7 %fusion.56 = f32[192,16,64]{0,2,1:T(8,128)S(1)} fusion(f32[16,512,192]{1,2,0:T(8,128)} %get-tuple-element.228, f32[192,16]{0,1:T(8,128)S(1)} %select_maximum_fusion.2, bf16[3072,16,2,64]{0,3,2,1:T(8,128)(2,1)} %get-tuple-element.257, s32[]{:T(128)S(6)} %select_n.18, s32[]{:T(128)S(6)} %add.95, f32[192,16,64]{0,2,1:T(8,128)S(1)} %get-tuple-element.245, ...), kind=kOutput, calls=%fused_computation.9.clone.1 | convolution fusion | flops 206635008 | bytes 8937481 | tf_op jit(solution)/shard_map/while/body/eval_jaxpr/thk,khd->thd/dot_general | solution.py:30
  319.5 4.9 %bitcast_reduce_fusion.2 = (f32[192,16]{0,1:T(8,128)S(1)}, f32[16,512,192]{1,2,0:T(8,128)}) fusion(bf16[192,16,64]{0,2,1:T(8,128)(2,1)S(1)} %get-tuple-element.258, bf16[3072,16,2,64]{0,3,2,1:T(8,128)(2,1)} %get-tuple-element.257, s32[]{:T(128)S(6)} %select_n.18), kind=kOutput, calls=%fused_computation.1.clone.1 | convolution fusion | flops 204469248 | bytes 7745540 | tf_op jit(solution)/shard_map/while/body/eval_jaxpr/thd,khd->thk/dot_general | solution.py:22
  324.4 3.6 %fusion.54 = f32[192,16]{0,1:T(8,128)S(1)} fusion(f32[16,512,192]{1,2,0:T(8,128)} %get-tuple-element.228, f32[192,16]{0,1:T(8,128)S(1)} %select_maximum_fusion.2), kind=kLoop, calls=%fused_computation.4.clone.1 | loop fusion | flops 4715520 | bytes 6316032 | tf_op jit(solution)/shard_map/while/body/eval_jaxpr/reduce_sum | solution.py:29
  328.1 4.7 %fusion.56 = f32[192,16,64]{0,2,1:T(8,128)S(1)} fusion(f32[16,512,192]{1,2,0:T(8,128)} %get-tuple-element.228, f32[192,16]{0,1:T(8,128)S(1)} %select_maximum_fusion.2, bf16[3072,16,2,64]{0,3,2,1:T(8,128)(2,1)} %get-tuple-element.257, s32[]{:T(128)S(6)} %select_n.18, s32[]{:T(128)S(6)} %add.95, f32[192,16,64]{0,2,1:T(8,128)S(1)} %get-tuple-element.245, ...), kind=kOutput, calls=%fused_computation.9.clone.1 | convolution fusion | flops 206635008 | bytes 8937481 | tf_op jit(solution)/shard_map/while/body/eval_jaxpr/thk,khd->thd/dot_general | solution.py:30
  332.8 0.2 fusion.26
  333.0 0.3 fusion.23
  333.3 2.9 fusion.25
  (35 shorter events, 0.2 us)
Async XLA Ops:
  6.5 34.8 %copy-start = (bf16[1,51,1024]{2,1,0:T(8,128)(2,1)S(1)}, bf16[1,51,1024]{2,1,0:T(8,128)(2,1)}, u32[]{:S(2)}) copy-start(bf16[1,51,1024]{2,1,0:T(8,128)(2,1)} %param.14) | copy-start | bytes 313348
  6.5 34.8 %all-gather.6.cloned.1.call-start = ((), (), s32[]{:S(2)}) async-start(), calls=%async_computation | async-start | bytes 9437184 | tf_op jit(solution)/shard_map/all_gather | solution.py:60
  7.3 229.1 %all-gather.8.cloned.1.call-start = ((), (), s32[]{:S(2)}) async-start(), calls=%async_computation.1 | async-start | bytes 13369344 | tf_op jit(solution)/shard_map/all_gather | solution.py:81
  41.3 8.7 %copy-start.2 = (s32[1,1,192]{2,1,0:T(1,128)S(1)}, s32[1,1,192]{2,1,0:T(1,128)}, u32[]{:S(2)}) copy-start(s32[1,1,192]{2,1,0:T(1,128)} %param.13) | copy-start | bytes 2308
  50.0 283.4 %all-gather.10.cloned.1.call-start = ((), (), s32[]{:S(2)}) async-start(), calls=%async_computation.2 | async-start | bytes 3145728 | tf_op jit(solution)/shard_map/all_gather | solution.py:103
  50.2 3.0 collective-permute-start.1
  87.4 10.5 %collective-permute-start = (bf16[4,2048]{1,0:T(4,128)(2,1)S(1)}, bf16[4,2048]{1,0:T(4,128)(2,1)S(1)}, u32[]{:S(2)}, u32[]{:S(2)}) collective-permute-start(bf16[4,2048]{1,0:T(4,128)(2,1)S(1)} %fusion.18), channel_id=1, source_target_pairs={{0,1},{1,0},{2,3},{3,2},{4,5},{5,4},{6,7},{7,6},{8,9},{9,8},{10,11... | collective-permute-start | bytes 49160 | tf_op jit(solution)/shard_map/ppermute | solution.py:16
  253.1 79.9 %copy-start.1 = (bf16[64,16,1,64]{0,3,1,2:T(8,128)(2,1)S(1)}, bf16[64,16,1,64]{0,3,1,2:T(8,128)(2,1)}, u32[]{:S(2)}) copy-start(bf16[64,16,1,64]{0,3,1,2:T(8,128)(2,1)} %copy.45) | copy-start | bytes 393220
Sparse Core Ops, SparseCore 0:
  9.4 31.8 all-gather.5
  50.1 186.2 all-gather.7
  238.5 16.4 all-gather.9
where the time goes:
time: 344 us; the launch traced here: 343 us
  waiting for transfers between devices  138 us (40%)
  matrix products  66.9 us (19%)
  blocking collectives  64.6 us (19%)
  local copies, waits for them, and re-layouts  24.3 us (7%)
  other arithmetic  23.8 us (7%)
  between operations  13.3 us (4%)
  starting transfers between devices  11.6 us (3%)
    all_gather x1, waiting for transfers between devices, shards(): portion = lax.all_gather(key_values, 'peak', axis=0, tiled=True)  104 us
    all_gather x1, blocking collectives, shards(): bias_part = lax.all_gather(partner_bias, 'peak', axis=0, tiled=True)  33.7 us
    all_gather x1, waiting for transfers between devices, shards(): lax.all_gather(qkv_weight, 'mod', axis=0, tiled=True)  32.6 us
    all_gather x1, blocking collectives, shards(): kv_part = lax.all_gather(partner_kv, 'peak', axis=0, tiled=True)  31 us
    dot_general x7, matrix products, attend_block(): jnp.einsum('thd,khd->thk', queries, key_block, preferred_element_type=jnp...  30.7 us
    dot_general x7, matrix products, attend_block(): jnp.einsum('thk,khd->thd', weights.astype(jnp.bfloat16), value_block, pre...  28.4 us
    reduce_sum x7, other arithmetic, attend_block(): denominator = denominator * correction + jnp.sum(weights, axis=2)  22.1 us
    all_gather x1, local copies, waits for them, and re-layouts, shards(): portion = lax.all_gather(key_values, 'peak', axis=0, tiled=True)  16.7 us
  transfers between devices with their start and end apart: 5, of which 3 were waited for; matrix products, arithmetic and copies ran while one was open for 30% of the time, Pallas kernels for 0%

commit v1 on v0

v1 whole, which is shorter than its diff:
```python
import functools

import jax
import jax.numpy as jnp
from jax import lax
from jax.experimental import pallas as pl
from jax.experimental.pallas import tpu as pltpu
from jax.sharding import PartitionSpec as P

H = 16
NBINS = 51
TOK = 192
HALF = TOK // 2
WIDTH = 1024
NP = 16
PAIRS = 8
SELF = 8
GROUP = 4
CHUNK = 384
MESH = pl.DeviceIdType.MESH
F32 = jnp.float32
BF16 = jnp.bfloat16


def dot(a, b):
    return jnp.dot(a, b, preferred_element_type=F32)


def dot_t(a, b):
    return lax.dot_general(a, b, (((1,), (1,)), ((), ())), preferred_element_type=F32)


def low_lanes(rows):
    return lax.broadcasted_iota(jnp.int32, (rows, 128), 1) < 64


def kernel(
    hid, bins, flags, seg, tab, mvec, w, wo, out,
    e_scr, tab_scr, w_own, w_oth, wo_scr, kvs, kvr, qs, qr, pls, plx, plr,
    vt, pk_scr, pvt_scr, bias_scr, qz, s_scr, os, att, acc,
    w_sem, wx_ssem, wx_rsem, wo_sem, wox_ssem, wox_rsem,
    kv_ssem, kv_rsem, q_ssem, q_rsem, px_ssem, px_rsem, pl_ssem, pl_rsem, b_ssem, b_rsem,
):
    p = lax.axis_index("peak")
    m = lax.axis_index("mod")
    z = p // 2
    xh = lax.rem(p, 2)
    other = 1 - m

    def target(i, dx):
        return 2 * lax.rem(z + 4 + i, PAIRS) + lax.rem(xh + dx, 2)

    def source(i, dx):
        return 2 * lax.rem(z + 12 - i, PAIRS) + lax.rem(xh + dx, 2)

    def to_peer(src, dst, ssem, rsem, t):
        return pltpu.make_async_remote_copy(
            src, dst, ssem, rsem, device_id={"peak": t}, device_id_type=MESH
        )

    def to_partner(src, dst, ssem, rsem):
        return pltpu.make_async_remote_copy(
            src, dst, ssem, rsem, device_id={"mod": other}, device_id_type=MESH
        )

    def kv_copy(i, dx):
        k = 2 * i + dx
        t = target(i, dx)
        return to_peer(kvs.at[t], kvr.at[k], kv_ssem.at[k], kv_rsem.at[k], t)

    def q_copy(i, dx):
        k = 2 * i + dx
        t = target(i, dx)
        return to_peer(qs.at[t], qr.at[k], q_ssem.at[k], q_rsem.at[k], t)

    def pool_copy(i, dx):
        k = 2 * i + dx
        t = target(i, dx)
        return to_peer(plx.at[t], plr.at[k], pl_ssem.at[k], pl_rsem.at[k], t)

    def back_copy(i, dx):
        k = 2 * i + dx
        return to_peer(os.at[k], att.at[p], b_ssem.at[k], b_rsem.at[k], source(i, dx))

    def pool_swap(i):
        j = lax.rem(z + 4 + i, PAIRS)
        return to_partner(
            pls.at[pl.ds(2 * j, 2)], plx.at[pl.ds(2 * j, 2)], px_ssem.at[i], px_rsem.at[i]
        )

    def columns(i):
        j = lax.rem(z + 4 + i, PAIRS)
        return w.at[:, pl.ds(pl.multiple_of(j * 384, 128), 384)]

    def w_copy(i):
        return pltpu.make_async_copy(columns(i), w_own.at[i], w_sem.at[i])

    def w_swap(i):
        return to_partner(columns(i), w_oth.at[i], wx_ssem.at[i], wx_rsem.at[i])

    own_rows = pl.ds(pl.multiple_of(m * 512, 512), 512)
    oth_rows = pl.ds(pl.multiple_of(other * 512, 512), 512)
    wo_copy = pltpu.make_async_copy(wo, wo_scr.at[own_rows], wo_sem)
    wo_swap = to_partner(wo, wo_scr.at[own_rows], wox_ssem, wox_rsem)

    barrier = pltpu.get_barrier_semaphore()
    for i in range(PAIRS):
        for dx in range(2):
            if 2 * i + dx != SELF:
                pl.semaphore_signal(
                    barrier, inc=1, device_id={"peak": target(i, dx)}, device_id_type=MESH
                )
    pl.semaphore_signal(barrier, inc=1, device_id={"mod": other}, device_id_type=MESH)

    for i in range(PAIRS):
        w_copy(i).start()
    wo_copy.start()

    tab_scr[...] = jnp.zeros_like(tab_scr)
    tab_scr[0:NBINS] = tab[0]
    row = lax.broadcasted_iota(jnp.int32, (128, TOK), 0)
    onehot = jnp.where(row < 64, (row == bins[...]).astype(F32), (flags[...] == 1).astype(F32))
    picked = onehot.T
    rows_of_bin = dot(picked[:, :64].astype(BF16), tab_scr[...])
    masked = picked[:, 64:65] > 0.5
    chosen = jnp.where(masked, mvec[...].astype(F32), hid[0].astype(F32))
    e_scr[...] = (chosen + rows_of_bin).astype(BF16)

    segment = jnp.bitwise_and(lax.broadcasted_iota(jnp.int32, (16, TOK), 0), 3)
    chosen_seg = (segment == seg[0]).astype(F32)
    counts = jnp.sum(chosen_seg, axis=1, keepdims=True)
    log_counts = jnp.broadcast_to(jnp.log(counts), (16, 128))
    sel = chosen_seg.astype(BF16)
    pool_row = lax.broadcasted_iota(jnp.int32, (16, 128), 0) < 4

    pl.semaphore_wait(barrier, 16)
    for i in range(PAIRS):
        w_swap(i).start()
    wo_swap.start()

    lo = low_lanes(TOK)
    lo_half = low_lanes(HALF)

    def project(i, carry):
        j = lax.rem(z + 4 + i, PAIRS)
        w_copy(i).wait()
        w_swap(i).wait_recv()
        pr = dot(e_scr[:, own_rows], w_own[i]) + dot(e_scr[:, oth_rows], w_oth[i])
        t0, t1, t2 = pr[:, 0:128], pr[:, 128:256], pr[:, 256:384]
        r0 = pltpu.roll(t0, 64, 1)
        r1 = pltpu.roll(t1, 64, 1)
        kv0 = jnp.where(lo, r0, r1).astype(BF16)
        kv1 = t2.astype(BF16)
        kvs[2 * j] = kv0
        kvs[2 * j + 1] = kv1
        for dx in range(2):
            @pl.when(2 * i + dx != SELF)
            def _():
                kv_copy(i, dx).start()
        q0 = jnp.where(lo_half, t0[:HALF], r0[HALF:])
        q1 = jnp.where(lo_half, r1[:HALF], t1[HALF:])
        qs[2 * j] = (q0 * 0.125).astype(BF16)
        qs[2 * j + 1] = (q1 * 0.125).astype(BF16)
        pls[2 * j] = jnp.where(pool_row, dot(sel, kv0) / counts, log_counts).astype(BF16)
        pls[2 * j + 1] = jnp.where(pool_row, dot(sel, kv1) / counts, log_counts).astype(BF16)
        pool_swap(i).start()
        return carry

    lax.fori_loop(0, PAIRS, project, 0)
    kvr[SELF] = kvs[p]
    qr[SELF] = qs[p]

    def forward(i, carry):
        pool_swap(i).wait_recv()
        for dx in range(2):
            @pl.when(2 * i + dx != SELF)
            def _():
                pool_copy(i, dx).start()
        return carry

    lax.fori_loop(0, PAIRS, forward, 0)
    plr[SELF] = plx[p]

    def send_q(i, carry):
        for dx in range(2):
            @pl.when(2 * i + dx != SELF)
            def _():
                q_copy(i, dx).start()
        return carry

    lax.fori_loop(0, PAIRS, send_q, 0)

    def take_values(i, carry):
        for dx in range(2):
            @pl.when(2 * i + dx != SELF)
            def _():
                kv_copy(i, dx).wait_recv()
        block = kvr[pl.ds(2 * i, 2)].reshape(2 * TOK, 128).astype(F32).T
        vt[:, pl.ds(pl.multiple_of(i * 384, 128), 384)] = block[64:128].astype(BF16)
        return carry

    lax.fori_loop(0, PAIRS, take_values, 0)

    def take_pooled(i, carry):
        for dx in range(2):
            @pl.when(2 * i + dx != SELF)
            def _():
                pool_copy(i, dx).wait_recv()
        return carry

    lax.fori_loop(0, PAIRS, take_pooled, 0)
    pooled = plr[...].reshape(NP * 16, 128)
    summary = lax.broadcasted_iota(jnp.int32, (64, 256), 0)
    place = (summary // 4) * 16 + jnp.bitwise_and(summary, 3)
    column = lax.broadcasted_iota(jnp.int32, (64, 256), 1)
    pk = dot((column == place).astype(BF16), pooled)
    pk_scr[...] = pk.astype(BF16)
    bias_scr[...] = dot((column == place + 4).astype(BF16), pooled)
    pk_pad = jnp.concatenate([pk, jnp.zeros((64, 128), F32)], axis=0).T
    pvt_scr[...] = pk_pad[64:128].astype(BF16)

    cols = GROUP * TOK
    n_chunks = NP * TOK // CHUNK

    def attend(g, carry):
        for kk in range(GROUP):
            i = g * (GROUP // 2) + kk // 2
            dx = kk % 2

            @pl.when(2 * i + dx != SELF)
            def _():
                q_copy(i, dx).wait_recv()
            a = qr[2 * i + dx].astype(F32)
            top = jnp.where(lo_half, a, 0.0)
            bottom = jnp.where(lo_half, pltpu.roll(a, 64, 1), 0.0)
            qz[kk * TOK:kk * TOK + HALF] = top.astype(BF16)
            qz[kk * TOK + HALF:(kk + 1) * TOK] = bottom.astype(BF16)
        s_pool = dot_t(pk_scr[...], qz[...]) + bias_scr[:, 0:1]
        m8 = jnp.max(s_pool.reshape(8, 8, cols), axis=0)

        def score(c, m8):
            keys = kvr[pl.ds(c * (CHUNK // TOK), CHUNK // TOK)].reshape(CHUNK, 128)
            s = dot_t(keys, qz[...])
            s_scr[pl.ds(pl.multiple_of(c * CHUNK, CHUNK), CHUNK)] = s
            return jnp.maximum(m8, jnp.max(s.reshape(CHUNK // 8, 8, cols), axis=0))

        m8 = lax.fori_loop(0, n_chunks, score, m8)
        top_score = jnp.max(m8, axis=0, keepdims=True)
        w_pool = jnp.exp(s_pool - top_score)
        l8 = jnp.sum(w_pool.reshape(8, 8, cols), axis=0)
        acc_o = dot(pvt_scr[:, 0:64], w_pool.astype(BF16))

        def weigh(c, state):
            l8, acc_o = state
            s = s_scr[pl.ds(pl.multiple_of(c * CHUNK, CHUNK), CHUNK)]
            wt = jnp.exp(s - top_score)
            l8 = l8 + jnp.sum(wt.reshape(CHUNK // 8, 8, cols), axis=0)
            values = vt[:, pl.ds(pl.multiple_of(c * CHUNK, 128), CHUNK)]
            return l8, acc_o + dot(values, wt.astype(BF16))

        l8, acc_o = lax.fori_loop(0, n_chunks, weigh, (l8, acc_o))
        attended = (acc_o / jnp.sum(l8, axis=0, keepdims=True)).T
        for kk in range(GROUP):
            i = g * (GROUP // 2) + kk // 2
            dx = kk % 2
            rows = attended[kk * TOK:(kk + 1) * TOK]
            packed = jnp.concatenate([rows[:HALF], rows[HALF:]], axis=1).astype(BF16)
            os[2 * i + dx] = packed

            @pl.when(2 * i + dx != SELF)
            def _():
                back_copy(i, dx).start()

            @pl.when(2 * i + dx == SELF)
            def _():
                att[p] = packed
        return carry

    lax.fori_loop(0, NP // GROUP, attend, 0)

    wo_copy.wait()
    wo_swap.wait_recv()
    acc[...] = jnp.zeros_like(acc)

    def finish(i, carry):
        j = lax.rem(z + 4 + i, PAIRS)
        for dx in range(2):
            @pl.when(2 * i + dx != SELF)
            def _():
                back_copy(i, dx).wait_recv()
        a = att[2 * j].astype(F32)
        b = att[2 * j + 1].astype(F32)
        top = jnp.where(lo_half, a, pltpu.roll(b, 64, 1))
        bottom = jnp.where(lo_half, pltpu.roll(a, 64, 1), b)
        rows = jnp.concatenate([top, bottom], axis=0).astype(BF16)
        acc[...] += dot(rows, wo_scr[pl.ds(pl.multiple_of(j * 128, 128), 128)])
        return carry

    lax.fori_loop(0, PAIRS, finish, 0)
    out[0] = acc[...].astype(BF16)

    def drain(i, carry):
        for dx in range(2):
            @pl.when(2 * i + dx != SELF)
            def _():
                kv_copy(i, dx).wait_send()
                q_copy(i, dx).wait_send()
                pool_copy(i, dx).wait_send()
                back_copy(i, dx).wait_send()
        pool_swap(i).wait_send()
        w_swap(i).wait_send()
        return carry

    lax.fori_loop(0, PAIRS, drain, 0)
    wo_swap.wait_send()


def shards(hidden_in, value_bins, mask_flags, segment_ids, bin_table, mask_vector, qkv_weight, out_weight):
    vmem = pl.BlockSpec(memory_space=pltpu.VMEM)
    hbm = pl.BlockSpec(memory_space=pl.ANY)
    dma = pltpu.SemaphoreType.DMA
    return pl.pallas_call(
        kernel,
        out_shape=jax.ShapeDtypeStruct((1, TOK, WIDTH), BF16),
        in_specs=[vmem] * 6 + [hbm] * 2,
        out_specs=vmem,
        scratch_shapes=[
            pltpu.VMEM((TOK, WIDTH), BF16),
            pltpu.VMEM((64, WIDTH), BF16),
            pltpu.VMEM((PAIRS, 512, 384), BF16),
            pltpu.VMEM((PAIRS, 512, 384), BF16),
            pltpu.VMEM((WIDTH, WIDTH), BF16),
            pltpu.VMEM((NP, TOK, 128), BF16),
            pltpu.VMEM((NP, TOK, 128), BF16),
            pltpu.VMEM((NP, HALF, 128), BF16),
            pltpu.VMEM((NP, HALF, 128), BF16),
            pltpu.VMEM((NP, 16, 128), BF16),
            pltpu.VMEM((NP, 16, 128), BF16),
            pltpu.VMEM((NP, 16, 128), BF16),
            pltpu.VMEM((64, NP * TOK), BF16),
            pltpu.VMEM((64, 128), BF16),
            pltpu.VMEM((64, 128), BF16),
            pltpu.VMEM((64, 128), F32),
            pltpu.VMEM((GROUP * TOK, 128), BF16),
            pltpu.VMEM((NP * TOK, GROUP * TOK), F32),
            pltpu.VMEM((NP, HALF, 128), BF16),
            pltpu.VMEM((NP, HALF, 128), BF16),
            pltpu.VMEM((TOK, WIDTH), F32),
            dma((PAIRS,)), dma((PAIRS,)), dma((PAIRS,)),
            dma, dma, dma,
            dma((NP,)), dma((NP,)), dma((NP,)), dma((NP,)),
            dma((PAIRS,)), dma((PAIRS,)), dma((NP,)), dma((NP,)), dma((NP,)), dma((NP,)),
        ],
        compiler_params=pltpu.CompilerParams(
            collective_id=0, has_side_effects=True, vmem_limit_bytes=50 << 20
        ),
        cost_estimate=pl.CostEstimate(
            flops=4 * 10**9, bytes_accessed=10 * 2**20, transcendentals=10**7
        ),
    )(hidden_in, value_bins, mask_flags, segment_ids, bin_table, mask_vector, qkv_weight, out_weight)


def solution(mesh):
    placed = (
        P("mod", ("dp", "peak"), None),
        P("mod", ("dp", "peak")),
        P("mod", ("dp", "peak")),
        P("mod", ("dp", "peak"), None),
        P("mod", None, None),
        P("mod", None),
        P("mod", None),
        P("mod", None),
    )
    return jax.shard_map(
        shards,
        mesh=mesh,
        in_specs=placed,
        out_specs=P("mod", ("dp", "peak"), None),
        check_vma=False,
    )
```

time: 344 us -> 84.9 us (0.25)
  waiting for transfers between devices: 138 us -> 0 us
  Pallas kernels: 0 us -> 78 us
  matrix products: 66.9 us -> 0 us
  blocking collectives: 64.6 us -> 0 us
  other arithmetic: 23.8 us -> 0 us
  local copies, waits for them, and re-layouts: 24.3 us -> 6.59 us
  between operations: 13.3 us -> 0.02 us
  starting transfers between devices: 11.6 us -> 0 us
    all_gather x3 -> x0, waiting for transfers between devices: 137 us -> none  [the longest x1 104 us: shards(): portion = lax.all_gather(key_values, 'peak', axis=0, tiled=True)]
    pallas_call x0 -> x1, Pallas kernels: none -> 78 us  [shards(): pl.pallas_call(kernel, out_shape=jax.ShapeDtypeStruct((1, TOK, WIDTH), BF...]
    dot_general x17 -> x0, matrix products: 66.9 us -> none  [the longest x7 30.7 us: attend_block(): jnp.einsum('thd,khd->thk', queries, key_block, preferred_element_type=jnp...]
    all_gather x2 -> x0, blocking collectives: 64.6 us -> none  [the longest x1 33.7 us: shards(): bias_part = lax.all_gather(partner_bias, 'peak', axis=0, tiled=True)]
    reduce_sum x8 -> x0, other arithmetic: 22.2 us -> none  [the longest x7 22.1 us: attend_block(): denominator = denominator * correction + jnp.sum(weights, axis=2)]
    all_gather x1 -> x0, local copies, waits for them, and re-layouts: 16.7 us -> none  [shards(): portion = lax.all_gather(key_values, 'peak', axis=0, tiled=True)]
    ppermute x2 -> x0, starting transfers between devices: 11.5 us -> none  [from_partner(): return lax.ppermute(value, axis, pairs)]
    unnamed x7 -> x15, local copies, waits for them, and re-layouts: 1.1 us -> 6.59 us
  transfers between devices with their start and end apart: 5 -> 0, of which waited for: 3 -> 0; matrix products, arithmetic and copies ran while one was open for 30% -> 0% of each run, Pallas kernels for 0% -> 0%
where the time goes in v1:
time: 84.9 us; the launch traced here: 84.6 us
  Pallas kernels  78 us (92%)
  local copies, waits for them, and re-layouts  6.59 us (8%)
    pallas_call x1, Pallas kernels, shards(): pl.pallas_call(kernel, out_shape=jax.ShapeDtypeStruct((1, TOK, WIDTH), BF...  78 us
    unnamed x15, local copies, waits for them, and re-layouts  6.59 us

profile of v1, /device:TPU:1, one launch (start us, length us, event | category | flops | bytes accessed | tf_op | source)
XLA Modules:
  0.0 84.6 jit_solution(12732864658900015348)
XLA Ops:
  0.0 0.0 copy-start
  0.0 1.2 %copy-done = bf16[512,1024]{1,0:T(8,128)(2,1)S(1)} copy-done((bf16[512,1024]{1,0:T(8,128)(2,1)S(1)}, bf16[512,1024]{1,0:T(8,128)(2,1)}, u32[]{:S(2)}) %copy-start) | copy-done | bytes 1048600
  1.2 0.0 copy-start.1
  1.2 1.0 %copy-done.1 = bf16[1,192,1024]{2,1,0:T(8,128)(2,1)S(1)} copy-done((bf16[1,192,1024]{2,1,0:T(8,128)(2,1)S(1)}, bf16[1,192,1024]{2,1,0:T(8,128)(2,1)}, u32[]{:S(2)}) %copy-start.1) | copy-done | bytes 393240
  2.2 0.0 copy-start.2
  2.2 0.9 %copy-done.2 = bf16[1,51,1024]{2,1,0:T(8,128)(2,1)S(1)} copy-done((bf16[1,51,1024]{2,1,0:T(8,128)(2,1)S(1)}, bf16[1,51,1024]{2,1,0:T(8,128)(2,1)}, u32[]{:S(2)}) %copy-start.2) | copy-done | bytes 104472
  3.1 0.0 copy-start.3
  3.1 0.7 copy-done.3
  3.8 0.0 copy-start.4
  3.8 0.7 copy-done.4
  4.5 0.0 copy-start.5
  4.5 0.7 copy-done.5
  5.2 0.0 copy-start.6
  5.2 0.7 copy-done.6
  5.8 78.0 %shard_map.82 = bf16[1,192,1024]{2,1,0:T(8,128)(2,1)S(1)} custom-call(bf16[1,192,1024]{2,1,0:T(8,128)(2,1)S(1)} %copy-done.1, s32[1,192]{1,0:T(1,128)S(1)} %copy-done.4, s32[1,192]{1,0:T(1,128)S(1)} %copy-done.5, s32[1,1,192]{2,1,0:T(1,128)S(1)} %copy-done.6, bf16[1,51,1024]{2,1,0:T(8,128)(2,1)S(1)} %copy-done.2, bf16[1,1024]{1,0:T(2,128)(2,1)S(1)} %copy-done.3, ...), custom_call_target="tpu_custom_call" | custom-call | flops 4000000000 | bytes 10485760 | tf_op jit(solution)/shard_map/pallas_call | solution.py:322
  83.8 0.7 copy.10
Async XLA Ops:
  0.0 1.2 %copy-start = (bf16[512,1024]{1,0:T(8,128)(2,1)S(1)}, bf16[512,1024]{1,0:T(8,128)(2,1)}, u32[]{:S(2)}) copy-start(bf16[512,1024]{1,0:T(8,128)(2,1)} %wo.1) | copy-start | bytes 3145732
  1.2 1.0 %copy-start.1 = (bf16[1,192,1024]{2,1,0:T(8,128)(2,1)S(1)}, bf16[1,192,1024]{2,1,0:T(8,128)(2,1)}, u32[]{:S(2)}) copy-start(bf16[1,192,1024]{2,1,0:T(8,128)(2,1)} %hid.1) | copy-start | bytes 1179652
  2.2 0.9 %copy-start.2 = (bf16[1,51,1024]{2,1,0:T(8,128)(2,1)S(1)}, bf16[1,51,1024]{2,1,0:T(8,128)(2,1)}, u32[]{:S(2)}) copy-start(bf16[1,51,1024]{2,1,0:T(8,128)(2,1)} %tab.1) | copy-start | bytes 313348
  3.1 0.7 copy-start.3
  3.8 0.7 copy-start.4
  4.5 0.7 copy-start.5
  5.2 0.7 copy-start.6

commit v2 on v1

--- a/solution.py
+++ b/solution.py
@@ -16,7 +16,7 @@
 PAIRS = 8
 SELF = 8
 GROUP = 4
-CHUNK = 384
+CHUNK = 3072
 MESH = pl.DeviceIdType.MESH
 F32 = jnp.float32
 BF16 = jnp.bfloat16
@@ -35,7 +35,8 @@
 
 
 def kernel(
-    hid, bins, flags, seg, tab, mvec, w, wo, out,
+    hid_in, bins_in, flags_in, seg_in, tab_in, mvec_in, w, wo, out,
+    hid, bins, flags, seg, tab, mvec, in_sem,
     e_scr, tab_scr, w_own, w_oth, wo_scr, kvs, kvr, qs, qr, pls, plx, plr,
     vt, pk_scr, pvt_scr, bias_scr, qz, s_scr, os, att, acc,
     w_sem, wx_ssem, wx_rsem, wo_sem, wox_ssem, wox_rsem,
@@ -112,9 +113,19 @@
                 )
     pl.semaphore_signal(barrier, inc=1, device_id={"mod": other}, device_id_type=MESH)
 
+    loads = [
+        pltpu.make_async_copy(source_ref, place, in_sem.at[n])
+        for n, (source_ref, place) in enumerate((
+            (bins_in, bins), (flags_in, flags), (tab_in, tab), (seg_in, seg), (mvec_in, mvec), (hid_in, hid)
+        ))
+    ]
+    for load in loads:
+        load.start()
     for i in range(PAIRS):
         w_copy(i).start()
     wo_copy.start()
+    for load in loads:
+        load.wait()
 
     tab_scr[...] = jnp.zeros_like(tab_scr)
     tab_scr[0:NBINS] = tab[0]
@@ -317,14 +328,21 @@
 
 def shards(hidden_in, value_bins, mask_flags, segment_ids, bin_table, mask_vector, qkv_weight, out_weight):
     vmem = pl.BlockSpec(memory_space=pltpu.VMEM)
-    hbm = pl.BlockSpec(memory_space=pl.ANY)
+    hbm = pl.BlockSpec(memory_space=pltpu.MemorySpace.HBM)
     dma = pltpu.SemaphoreType.DMA
     return pl.pallas_call(
         kernel,
         out_shape=jax.ShapeDtypeStruct((1, TOK, WIDTH), BF16),
-        in_specs=[vmem] * 6 + [hbm] * 2,
+        in_specs=[hbm] * 8,
         out_specs=vmem,
         scratch_shapes=[
+            pltpu.VMEM(hidden_in.shape, BF16),
+            pltpu.VMEM(value_bins.shape, jnp.int32),
+            pltpu.VMEM(mask_flags.shape, jnp.int32),
+            pltpu.VMEM(segment_ids.shape, jnp.int32),
+            pltpu.VMEM(bin_table.shape, BF16),
+            pltpu.VMEM(mask_vector.shape, BF16),
+            dma((6,)),
             pltpu.VMEM((TOK, WIDTH), BF16),
             pltpu.VMEM((64, WIDTH), BF16),
             pltpu.VMEM((PAIRS, 512, 384), BF16),
@@ -352,7 +370,7 @@
             dma((PAIRS,)), dma((PAIRS,)), dma((NP,)), dma((NP,)), dma((NP,)), dma((NP,)),
         ],
         compiler_params=pltpu.CompilerParams(
-            collective_id=0, has_side_effects=True, vmem_limit_bytes=50 << 20
+            collective_id=0, has_side_effects=True, vmem_limit_bytes=64 << 20
         ),
         cost_estimate=pl.CostEstimate(
             flops=4 * 10**9, bytes_accessed=10 * 2**20, transcendentals=10**7

time: 84.9 us -> 70.3 us (0.83)
  Pallas kernels: 78 us -> 68.4 us
  local copies, waits for them, and re-layouts: 6.59 us -> 1.77 us
    pallas_call x1, Pallas kernels: 78 us -> 68.4 us  [shards(): pl.pallas_call(kernel, out_shape=jax.ShapeDtypeStruct((1, TOK, WIDTH), BF...]
    unnamed x15 -> x1, local copies, waits for them, and re-layouts: 6.59 us -> 1.77 us
where the time goes in v2:
time: 70.3 us; the launch traced here: 70.1 us
  Pallas kernels  68.4 us (97%)
  local copies, waits for them, and re-layouts  1.77 us (3%)
    pallas_call x1, Pallas kernels, shards(): pl.pallas_call(kernel, out_shape=jax.ShapeDtypeStruct((1, TOK, WIDTH), BF...  68.4 us
    unnamed x1, local copies, waits for them, and re-layouts  1.77 us

profile of v2, /device:TPU:1, one launch (start us, length us, event | category | flops | bytes accessed | tf_op | source)
XLA Modules:
  0.0 70.1 jit_solution(531230116218539182)
XLA Ops:
  0.0 68.4 %shard_map.82 = bf16[1,192,1024]{2,1,0:T(8,128)(2,1)} custom-call(bf16[1,192,1024]{2,1,0:T(8,128)(2,1)} %hid_in.1, s32[1,192]{1,0:T(1,128)} %bins_in.1, s32[1,192]{1,0:T(1,128)} %flags_in.1, s32[1,1,192]{2,1,0:T(1,128)} %seg_in.1, bf16[1,51,1024]{2,1,0:T(8,128)(2,1)} %tab_in.1, bf16[1,1024]{1,0:T(2,128)(2,1)} %mvec_in.1, bf16[512,3072]{1,0:T(8,128)(2,1)} %w.1, ...), custom_call_target="tpu_custom_call" | custom-call | flops 4000000000 | bytes 10485760 | tf_op jit(solution)/shard_map/pallas_call | solution.py:333
  68.4 1.8 %copy.10 = bf16[1,192,1024]{2,1,0:T(8,128)(2,1)} copy(bf16[1,192,1024]{2,1,0:T(8,128)(2,1)} %shard_map.82) | data formatting | bytes 786432

commit v3 on v2

--- a/solution.py
+++ b/solution.py
@@ -14,7 +14,7 @@
 WIDTH = 1024
 NP = 16
 PAIRS = 8
-SELF = 8
+SELF = 2
 GROUP = 4
 CHUNK = 3072
 MESH = pl.DeviceIdType.MESH
@@ -38,7 +38,7 @@
     hid_in, bins_in, flags_in, seg_in, tab_in, mvec_in, w, wo, out,
     hid, bins, flags, seg, tab, mvec, in_sem,
     e_scr, tab_scr, w_own, w_oth, wo_scr, kvs, kvr, qs, qr, pls, plx, plr,
-    vt, pk_scr, pvt_scr, bias_scr, qz, s_scr, os, att, acc,
+    vt, pk_scr, pvt_scr, bias_scr, qz, s_scr, os, att,
     w_sem, wx_ssem, wx_rsem, wo_sem, wox_ssem, wox_rsem,
     kv_ssem, kv_rsem, q_ssem, q_rsem, px_ssem, px_rsem, pl_ssem, pl_rsem, b_ssem, b_rsem,
 ):
@@ -48,11 +48,18 @@
     xh = lax.rem(p, 2)
     other = 1 - m
 
+    def step(i):
+        near, odd = i // 2, i % 2
+        return 4 + (2 * odd - 1) * near + 4 * odd * ((3 - near) // 3)
+
+    def pair_at(i):
+        return lax.rem(z + step(i), PAIRS)
+
     def target(i, dx):
-        return 2 * lax.rem(z + 4 + i, PAIRS) + lax.rem(xh + dx, 2)
+        return 2 * pair_at(i) + lax.rem(xh + dx, 2)
 
     def source(i, dx):
-        return 2 * lax.rem(z + 12 - i, PAIRS) + lax.rem(xh + dx, 2)
+        return 2 * lax.rem(z + 16 - step(i), PAIRS) + lax.rem(xh + dx, 2)
 
     def to_peer(src, dst, ssem, rsem, t):
         return pltpu.make_async_remote_copy(
@@ -84,13 +91,13 @@
         return to_peer(os.at[k], att.at[p], b_ssem.at[k], b_rsem.at[k], source(i, dx))
 
     def pool_swap(i):
-        j = lax.rem(z + 4 + i, PAIRS)
+        j = pair_at(i)
         return to_partner(
             pls.at[pl.ds(2 * j, 2)], plx.at[pl.ds(2 * j, 2)], px_ssem.at[i], px_rsem.at[i]
         )
 
     def columns(i):
-        j = lax.rem(z + 4 + i, PAIRS)
+        j = pair_at(i)
         return w.at[:, pl.ds(pl.multiple_of(j * 384, 128), 384)]
 
     def w_copy(i):
@@ -153,7 +160,7 @@
     lo_half = low_lanes(HALF)
 
     def project(i, carry):
-        j = lax.rem(z + 4 + i, PAIRS)
+        j = pair_at(i)
         w_copy(i).wait()
         w_swap(i).wait_recv()
         pr = dot(e_scr[:, own_rows], w_own[i]) + dot(e_scr[:, oth_rows], w_oth[i])
@@ -192,14 +199,26 @@
     lax.fori_loop(0, PAIRS, forward, 0)
     plr[SELF] = plx[p]
 
-    def send_q(i, carry):
-        for dx in range(2):
-            @pl.when(2 * i + dx != SELF)
-            def _():
-                q_copy(i, dx).start()
-        return carry
-
-    lax.fori_loop(0, PAIRS, send_q, 0)
+    def sent_kv(i, carry):
+        for dx in range(2):
+            @pl.when(2 * i + dx != SELF)
+            def _():
+                kv_copy(i, dx).wait_send()
+        return carry
+
+    lax.fori_loop(0, PAIRS, sent_kv, 0)
+
+    def each_in(g, action):
+        for kk in range(GROUP):
+            i = g * (GROUP // 2) + kk // 2
+            dx = kk % 2
+
+            @pl.when(2 * i + dx != SELF)
+            def _():
+                action(i, dx)
+
+    each_in(0, lambda i, dx: q_copy(i, dx).start())
+    each_in(1, lambda i, dx: q_copy(i, dx).start())
 
     def take_values(i, carry):
         for dx in range(2):
@@ -234,13 +253,16 @@
     n_chunks = NP * TOK // CHUNK
 
     def attend(g, carry):
+        each_in(g, lambda i, dx: q_copy(i, dx).wait_recv())
+
+        @pl.when(g == 0)
+        def _():
+            each_in(2, lambda i, dx: q_copy(i, dx).start())
+            each_in(3, lambda i, dx: q_copy(i, dx).start())
         for kk in range(GROUP):
             i = g * (GROUP // 2) + kk // 2
             dx = kk % 2
 
-            @pl.when(2 * i + dx != SELF)
-            def _():
-                q_copy(i, dx).wait_recv()
             a = qr[2 * i + dx].astype(F32)
             top = jnp.where(lo_half, a, 0.0)
             bottom = jnp.where(lo_half, pltpu.roll(a, 64, 1), 0.0)
@@ -289,12 +311,9 @@
 
     lax.fori_loop(0, NP // GROUP, attend, 0)
 
-    wo_copy.wait()
-    wo_swap.wait_recv()
-    acc[...] = jnp.zeros_like(acc)
 
     def finish(i, carry):
-        j = lax.rem(z + 4 + i, PAIRS)
+        j = pair_at(i)
         for dx in range(2):
             @pl.when(2 * i + dx != SELF)
             def _():
@@ -304,17 +323,18 @@
         top = jnp.where(lo_half, a, pltpu.roll(b, 64, 1))
         bottom = jnp.where(lo_half, pltpu.roll(a, 64, 1), b)
         rows = jnp.concatenate([top, bottom], axis=0).astype(BF16)
-        acc[...] += dot(rows, wo_scr[pl.ds(pl.multiple_of(j * 128, 128), 128)])
+        e_scr[:, pl.ds(pl.multiple_of(j * 128, 128), 128)] = rows
         return carry
 
     lax.fori_loop(0, PAIRS, finish, 0)
-    out[0] = acc[...].astype(BF16)
+    wo_copy.wait()
+    wo_swap.wait_recv()
+    out[0] = dot(e_scr[...], wo_scr[...]).astype(BF16)
 
     def drain(i, carry):
         for dx in range(2):
             @pl.when(2 * i + dx != SELF)
             def _():
-                kv_copy(i, dx).wait_send()
                 q_copy(i, dx).wait_send()
                 pool_copy(i, dx).wait_send()
                 back_copy(i, dx).wait_send()
@@ -363,19 +383,24 @@
             pltpu.VMEM((NP * TOK, GROUP * TOK), F32),
             pltpu.VMEM((NP, HALF, 128), BF16),
             pltpu.VMEM((NP, HALF, 128), BF16),
-            pltpu.VMEM((TOK, WIDTH), F32),
             dma((PAIRS,)), dma((PAIRS,)), dma((PAIRS,)),
             dma, dma, dma,
             dma((NP,)), dma((NP,)), dma((NP,)), dma((NP,)),
             dma((PAIRS,)), dma((PAIRS,)), dma((NP,)), dma((NP,)), dma((NP,)), dma((NP,)),
         ],
         compiler_params=pltpu.CompilerParams(
-            collective_id=0, has_side_effects=True, vmem_limit_bytes=64 << 20
+            collective_id=0, has_side_effects=True, vmem_limit_bytes=48 << 20
         ),
         cost_estimate=pl.CostEstimate(
             flops=4 * 10**9, bytes_accessed=10 * 2**20, transcendentals=10**7
         ),
-    )(hidden_in, value_bins, mask_flags, segment_ids, bin_table, mask_vector, qkv_weight, out_weight)
+    )(*[
+        pltpu.with_memory_space_constraint(x, pltpu.MemorySpace.HBM)
+        for x in (
+            hidden_in, value_bins, mask_flags, segment_ids,
+            bin_table, mask_vector, qkv_weight, out_weight,
+        )
+    ])
 
 
 def solution(mesh):

time: 70.3 us -> 64.8 us (0.922)
  Pallas kernels: 68.4 us -> 63.9 us
  local copies, waits for them, and re-layouts: 1.77 us -> 0.75 us
    pallas_call x1, Pallas kernels: 68.4 us -> 63.9 us  [shards(): pl.pallas_call(kernel, out_shape=jax.ShapeDtypeStruct((1, TOK, WIDTH), BF...]
    unnamed x1, local copies, waits for them, and re-layouts: 1.77 us -> 0.75 us
where the time goes in v3:
time: 64.8 us; the launch traced here: 64.7 us
  Pallas kernels  63.9 us (99%)
  local copies, waits for them, and re-layouts  0.75 us (1%)
    pallas_call x1, Pallas kernels, shards(): pl.pallas_call(kernel, out_shape=jax.ShapeDtypeStruct((1, TOK, WIDTH), BF...  63.9 us

profile of v3, /device:TPU:1, one launch (start us, length us, event | category | flops | bytes accessed | tf_op | source)
XLA Modules:
  0.0 64.7 jit_solution(8820089251377959281)
XLA Ops:
  0.0 63.9 %shard_map.82 = bf16[1,192,1024]{2,1,0:T(8,128)(2,1)S(1)} custom-call(bf16[1,192,1024]{2,1,0:T(8,128)(2,1)} %hid_in.1, s32[1,192]{1,0:T(1,128)} %bins_in.1, s32[1,192]{1,0:T(1,128)} %flags_in.1, s32[1,1,192]{2,1,0:T(1,128)} %seg_in.1, bf16[1,51,1024]{2,1,0:T(8,128)(2,1)} %tab_in.1, bf16[1,1024]{1,0:T(2,128)(2,1)} %mvec_in.1, bf16[512,3072]{1,0:T(8,128)(2,1)} %w.1, ...), custom_call_target="tpu_custom_call" | custom-call | flops 4000000000 | bytes 10485760 | tf_op jit(solution)/shard_map/pallas_call | solution.py:353
  63.9 0.7 %copy.10 = bf16[1,192,1024]{2,1,0:T(8,128)(2,1)} copy(bf16[1,192,1024]{2,1,0:T(8,128)(2,1)S(1)} %shard_map.82) | data formatting | bytes 786432

commit v4 on v3

--- a/solution.py
+++ b/solution.py
@@ -312,21 +312,21 @@
     lax.fori_loop(0, NP // GROUP, attend, 0)
 
 
-    def finish(i, carry):
-        j = pair_at(i)
+    def take_back(i, carry):
         for dx in range(2):
             @pl.when(2 * i + dx != SELF)
             def _():
                 back_copy(i, dx).wait_recv()
+        return carry
+
+    lax.fori_loop(0, PAIRS, take_back, 0)
+    for j in range(PAIRS):
         a = att[2 * j].astype(F32)
         b = att[2 * j + 1].astype(F32)
         top = jnp.where(lo_half, a, pltpu.roll(b, 64, 1))
         bottom = jnp.where(lo_half, pltpu.roll(a, 64, 1), b)
-        rows = jnp.concatenate([top, bottom], axis=0).astype(BF16)
-        e_scr[:, pl.ds(pl.multiple_of(j * 128, 128), 128)] = rows
-        return carry
-
-    lax.fori_loop(0, PAIRS, finish, 0)
+        e_scr[0:HALF, j * 128:(j + 1) * 128] = top.astype(BF16)
+        e_scr[HALF:TOK, j * 128:(j + 1) * 128] = bottom.astype(BF16)
     wo_copy.wait()
     wo_swap.wait_recv()
     out[0] = dot(e_scr[...], wo_scr[...]).astype(BF16)

time: 64.8 us -> 64.9 us (level)
  no operation moved by 1% of the time
where the time goes in v4:
time: 64.9 us; the launch traced here: 64.7 us
  Pallas kernels  63.9 us (98%)
  local copies, waits for them, and re-layouts  0.75 us (1%)
    pallas_call x1, Pallas kernels, shards(): pl.pallas_call(kernel, out_shape=jax.ShapeDtypeStruct((1, TOK, WIDTH), BF...  63.9 us

profile of v4, /device:TPU:1, one launch (start us, length us, event | category | flops | bytes accessed | tf_op | source)
XLA Modules:
  0.0 64.7 jit_solution(9801906360149664387)
XLA Ops:
  0.0 63.9 %shard_map.82 = bf16[1,192,1024]{2,1,0:T(8,128)(2,1)S(1)} custom-call(bf16[1,192,1024]{2,1,0:T(8,128)(2,1)} %hid_in.1, s32[1,192]{1,0:T(1,128)} %bins_in.1, s32[1,192]{1,0:T(1,128)} %flags_in.1, s32[1,1,192]{2,1,0:T(1,128)} %seg_in.1, bf16[1,51,1024]{2,1,0:T(8,128)(2,1)} %tab_in.1, bf16[1,1024]{1,0:T(2,128)(2,1)} %mvec_in.1, bf16[512,3072]{1,0:T(8,128)(2,1)} %w.1, ...), custom_call_target="tpu_custom_call" | custom-call | flops 4000000000 | bytes 10485760 | tf_op jit(solution)/shard_map/pallas_call | solution.py:353
  63.9 0.7 %copy.10 = bf16[1,192,1024]{2,1,0:T(8,128)(2,1)} copy(bf16[1,192,1024]{2,1,0:T(8,128)(2,1)S(1)} %shard_map.82) | data formatting | bytes 786432
